TPU v7x, 32 devices: a whole 2x2x4 slice. The times are simulated.
32 devices in a mesh: groups: 2 (over y), space: 4 (over z), chan: 2 (over x), rep: 2 (over core).
Axes of the slice: x: 2, y: 2, z: 4, core: 2. Of those that a mesh axis runs over, the one named last changes fastest.
Arguments:
- volume: bfloat16 [4, 8, 32, 8, 128], P(('groups', 'rep'), 'space', 'chan'), parts along dimension 0, may hold values from -6 to 6
- early_weight: bfloat16 [3, 3, 3, 128, 128], replicated, may hold values from -0.109375 to 0.109375
- late_weight: bfloat16 [3, 3, 3, 128, 512], P(None, None, None, None, 'chan'), may hold values from -0.109375 to 0.109375
- cotangent: bfloat16 [4, 4, 16, 4, 512], P(('groups', 'rep'), 'space', None, None, 'chan'), parts along dimension 0, may hold values from -6 to 6
Outputs:
- grad_early: bfloat16 [6, 3, 3, 128, 128], P('groups'), parts along dimension 0
- grad_late: bfloat16 [6, 3, 3, 128, 512], P('groups', None, None, None, 'chan'), parts along dimension 0
- grad_volume: bfloat16 [4, 8, 32, 8, 128], P(('groups', 'rep'), 'space', 'chan'), parts along dimension 0
There are 2 independent parts, one for each index of `groups`. A program takes and returns all parts, laid end to end along the dimension named above; an argument that names none is the same for every part. Nothing has to cross between parts.
All inputs are finite; a program needn't handle non-finite values.
Results may differ from a plain program's by a relative error of at most 0.0065.
Values may be sent and summed in bfloat16 or wider, within the bound.
No kernel may reach another device: no remote copies, remote signals or barrier semaphores. Data moves between devices by JAX's collectives and lax.ppermute only.
A program may use at most 64 MiB of HBM per device.

v0:
```python
import math
import jax
import jax.numpy as jnp
from jax import lax
from jax.sharding import PartitionSpec as P


def padded_2(block, sides, width):
    for axis, dim in sides:
        count = lax.axis_size(axis)
        forward = [(i, i + 1) for i in range(count - 1)]
        backward = [(target, source) for source, target in forward]
        low = lax.ppermute(
            lax.slice_in_dim(block, block.shape[dim] - width, None, axis=dim), axis, forward
        )
        high = lax.ppermute(lax.slice_in_dim(block, 0, width, axis=dim), axis, backward)
        block = jnp.concatenate([low, block, high], axis=dim)
    return block


def gelu_tanh(value):
    return jax.nn.gelu(value, approximate=True)


def conv_padded(padded, weight):
    depth = padded.shape[1] - 2
    height = padded.shape[2] - 2
    length = padded.shape[3] - 2
    total = None
    for first in range(3):
        for second in range(3):
            for third in range(3):
                window = padded[
                    :, first : first + depth, second : second + height, third : third + length
                ]
                term = jnp.einsum(
                    "sxyzc,co->sxyzo",
                    window,
                    weight[first, second, third],
                    preferred_element_type=jnp.float32,
                )
                total = term if total is None else total + term
    return total


def kernel_grad(padded, delta):
    depth = delta.shape[1]
    height = delta.shape[2]
    length = delta.shape[3]
    planes = []
    for first in range(3):
        for second in range(3):
            for third in range(3):
                window = padded[
                    :, first : first + depth, second : second + height, third : third + length
                ]
                planes.append(
                    jnp.einsum("sxyzc,sxyzo->co", window, delta, preferred_element_type=jnp.float32)
                )
    stacked = jnp.stack(planes, axis=0)
    return stacked.reshape((3, 3, 3) + stacked.shape[1:])


def flipped(weight):
    return jnp.swapaxes(weight[::-1, ::-1, ::-1], 3, 4)


def pad_dims(field, dims):
    widths = [(1, 1) if place in dims else (0, 0) for place in range(field.ndim)]
    return jnp.pad(field, widths)


def pool_cells(field):
    s, x, y, z, c = field.shape
    return jnp.mean(field.reshape(s, x // 2, 2, y // 2, 2, z // 2, 2, c), axis=(2, 4, 6))


def spread_cells(field):
    s, x, y, z, c = field.shape
    wide = jnp.broadcast_to(field[:, :, None, :, None, :, None, :], (s, x, 2, y, 2, z, 2, c))
    return wide.reshape(s, 2 * x, 2 * y, 2 * z, c) * 0.125


def late_layer(joined, late_weight, cotangent):
    rim = padded_2(joined, (("space", 1),), 1)
    late_pad = pad_dims(rim, (2, 3))
    pre_late = conv_padded(late_pad, late_weight)
    delta_late = jax.vjp(gelu_tanh, pre_late)[1](cotangent.astype(jnp.float32))[0].astype(
        jnp.bfloat16
    )
    late_part = kernel_grad(late_pad, delta_late)
    delta_rim = padded_2(delta_late, (("space", 1),), 1)
    back_partial = conv_padded(pad_dims(delta_rim, (2, 3)), flipped(late_weight))
    return (back_partial, late_part)


def per_device(volume, early_weight, late_weight, cotangent):
    count = (
        cotangent.shape[0]
        * lax.axis_size("rep")
        * cotangent.shape[1]
        * lax.axis_size("space")
        * cotangent.shape[2]
        * cotangent.shape[3]
    )
    scale = 1.0 / math.sqrt(count)
    haloed = padded_2(volume, (("space", 1), ("chan", 2)), 1)
    padded_in = pad_dims(haloed, (3,))
    pre_early = conv_padded(padded_in, early_weight)
    pooled = pool_cells(gelu_tanh(pre_early)).astype(jnp.bfloat16)
    joined = lax.all_gather(pooled, "chan", axis=2, tiled=True)
    back_partial, late_part = late_layer(joined, late_weight, cotangent)
    back_rows = lax.psum_scatter(back_partial, "chan", scatter_dimension=2, tiled=True)
    delta_early = jax.vjp(gelu_tanh, pre_early)[1](spread_cells(back_rows))[0].astype(jnp.bfloat16)
    early_part = kernel_grad(padded_in, delta_early)
    delta_halo = padded_2(delta_early, (("space", 1), ("chan", 2)), 1)
    grad_volume = conv_padded(pad_dims(delta_halo, (3,)), flipped(early_weight)).astype(
        jnp.bfloat16
    )
    early_total = lax.psum(early_part, ("space", "chan", "rep"))
    grad_early = (early_total * scale).astype(jnp.bfloat16)
    late_total = lax.psum(late_part, ("space", "rep"))
    grad_late = (late_total * scale).astype(jnp.bfloat16)
    return (grad_early, grad_late, grad_volume)


def solution(mesh):
    return jax.shard_map(
        per_device,
        mesh=mesh,
        in_specs=(
            P(("groups", "rep"), "space", "chan", None, None),
            P(),
            P(None, None, None, None, "chan"),
            P(("groups", "rep"), "space", None, None, "chan"),
        ),
        out_specs=(
            P("groups", None, None, None, None),
            P("groups", None, None, None, "chan"),
            P(("groups", "rep"), "space", "chan", None, None),
        ),
        check_vma=False,
    )
```

profile of v0, /device:TPU:0, one launch (start us, length us, event | category | flops | bytes accessed | tf_op | source)
XLA Modules:
  0.0 279.8 jit_solution(17251219886939649005)
XLA Ops:
  7.2 0.8 fusion.308
  8.0 4.9 %collective-permute-start = (bf16[1,1,16,8,128]{4,3,2,1,0:T(8,128)(2,1)S(1)}, bf16[1,1,16,8,128]{4,3,2,1,0:T(8,128)(2,1)S(1)}, u32[]{:S(2)}, u32[]{:S(2)}) collective-permute-start(bf16[1,1,16,8,128]{4,3,2,1,0:T(8,128)(2,1)S(1)} %get-tuple-element.12), channel_id=1, source_target_pairs={{0,4},{4,8},{8,12},{1,5},{5,9},{9,13},{2,6},{6,10},{10,14},{3,7},{... | collective-permute-start | bytes 98312 | tf_op jit(solution)/shard_map/ppermute | solution.py:13
  12.9 1.4 collective-permute-start.1
  14.4 3.8 %copy.129 = bf16[3,3,3,128,256]{3,4,2,1,0:T(8,128)(2,1)} copy(bf16[3,3,3,128,256]{4,3,2,1,0:T(8,128)(2,1)} %param.6) | data formatting | bytes 3538944 | tf_op args[2]
  18.2 0.6 collective-permute-done.1
  18.9 3.4 %collective-permute-start.2 = (bf16[1,4,1,8,128]{4,3,2,1,0:T(8,128)(2,1)S(1)}, bf16[1,4,1,8,128]{4,3,2,1,0:T(8,128)(2,1)S(1)}, u32[]{:S(2)}, u32[]{:S(2)}) collective-permute-start(bf16[1,4,1,8,128]{4,3,2,1,0:T(8,128)(2,1)S(1)} %get-tuple-element.7), channel_id=1, source_target_pairs={{0,2},{1,3},{4,6},{5,7},{8,10},{9,11},{12,14},{13,15},{16,18},{17,... | collective-permute-start | bytes 24584 | tf_op jit(solution)/shard_map/ppermute | solution.py:13
  22.3 1.4 collective-permute-start.3
  23.7 1.6 reverse_bitcast_fusion
  25.3 1.7 copy.133
  27.0 1.0 collective-permute-done.3
  32.5 4.5 %all-gather = bf16[16,4,128]{2,0,1:T(8,128)(2,1)S(1)} all-gather(bf16[8,4,128]{2,0,1:T(8,128)(2,1)S(1)} %fusion.279), channel_id=2, replica_groups=mesh['groups'=2,'space'=4,'chan'=2,'rep'=2] {'chan'}, dimensions={0}, use_global_device_ids=true | all-gather | bytes 24576 | tf_op jit(solution)/shard_map/all_gather | solution.py:111
  37.0 3.9 %collective-permute-start.4 = (bf16[1,1,16,4,128]{4,2,3,1,0:T(8,128)(2,1)S(1)}, bf16[1,1,16,4,128]{4,2,3,1,0:T(8,128)(2,1)S(1)}, u32[]{:S(2)}, u32[]{:S(2)}) collective-permute-start(bf16[1,1,16,4,128]{4,2,3,1,0:T(8,128)(2,1)S(1)} %bitcast.1506), channel_id=1, source_target_pairs={{0,4},{4,8},{8,12},{1,5},{5,9},{9,13},{2,6},{6,10},{10,14},{3,7},{... | collective-permute-start | bytes 49160 | tf_op jit(solution)/shard_map/ppermute | solution.py:13
  41.0 1.3 collective-permute-start.5
  42.3 1.2 reverse_bitcast_fusion.1
  43.5 3.1 %collective-permute-done.5 = bf16[1,1,16,4,128]{4,2,3,1,0:T(8,128)(2,1)S(1)} collective-permute-done((bf16[1,1,16,4,128]{4,2,3,1,0:T(8,128)(2,1)S(1)}, bf16[1,1,16,4,128]{4,2,3,1,0:T(8,128)(2,1)S(1)}, u32[]{:S(2)}, u32[]{:S(2)}) %collective-permute-start.5) | collective-permute-done | bytes 16416 | tf_op jit(solution)/shard_map/ppermute | solution.py:16
  50.5 3.5 %collective-permute-start.6 = (bf16[1,1,16,4,256]{4,2,3,1,0:T(8,128)(2,1)S(1)}, bf16[1,1,16,4,256]{4,2,3,1,0:T(8,128)(2,1)S(1)}, u32[]{:S(2)}, u32[]{:S(2)}) collective-permute-start(bf16[1,1,16,4,256]{4,2,3,1,0:T(8,128)(2,1)S(1)} %fusion.92), channel_id=1, source_target_pairs={{0,4},{4,8},{8,12},{1,5},{5,9},{9,13},{2,6},{6,10},{10,14},{3,7},{... | collective-permute-start | bytes 98312 | tf_op jit(solution)/shard_map/ppermute | solution.py:13
  54.0 1.3 collective-permute-start.7
  60.1 1.8 copy-done.1
  65.6 0.8 fusion.64
  66.5 0.9 fusion.2
  67.3 10.6 %reduce-scatter.2.cloned.1.call-done = f32[1,1,8,4,128]{4,2,3,1,0:T(8,128)} async-done(((f32[1,1,16,4,128]{4,2,3,1,0:T(8,128)}), f32[1,1,8,4,128]{4,2,3,1,0:T(8,128)}) %reduce-scatter.2.cloned.1.call-update) | async-done | bytes 16400 | tf_op jit(solution)/shard_map/reduce_scatter | solution.py:113
  77.9 0.7 multiply_bitcast_fusion.1
  79.1 0.9 fusion.60
  80.0 0.2 fusion.59
  80.4 0.2 fusion.57
  80.7 0.2 fusion.56
  81.8 0.2 fusion.51
  82.0 0.2 fusion.50
  82.7 0.2 fusion.47
  83.4 0.2 fusion.44
  83.8 0.2 fusion.42
  84.0 0.2 fusion.41
  84.5 0.2 fusion.39
  84.7 0.2 fusion.38
  85.6 1.2 copy-done.4
  87.0 3.4 %collective-permute-start.8 = (bf16[1,1,16,8,128]{4,3,2,1,0:T(8,128)(2,1)S(1)}, bf16[1,1,16,8,128]{4,3,2,1,0:T(8,128)(2,1)S(1)}, u32[]{:S(2)}, u32[]{:S(2)}) collective-permute-start(bf16[1,1,16,8,128]{4,3,2,1,0:T(8,128)(2,1)S(1)} %get-tuple-element.9), channel_id=1, source_target_pairs={{0,4},{4,8},{8,12},{1,5},{5,9},{9,13},{2,6},{6,10},{10,14},{3,7},{... | collective-permute-start | bytes 98312 | tf_op jit(solution)/shard_map/ppermute | solution.py:13
  90.4 1.3 collective-permute-start.9
  91.7 0.9 fusion.1
  92.6 3.8 %collective-permute-done.9 = bf16[1,1,16,8,128]{4,3,2,1,0:T(8,128)(2,1)S(1)} collective-permute-done((bf16[1,1,16,8,128]{4,3,2,1,0:T(8,128)(2,1)S(1)}, bf16[1,1,16,8,128]{4,3,2,1,0:T(8,128)(2,1)S(1)}, u32[]{:S(2)}, u32[]{:S(2)}) %collective-permute-start.9) | collective-permute-done | bytes 32800 | tf_op jit(solution)/shard_map/ppermute | solution.py:16
  96.4 2.7 collective-permute-start.10
  99.1 1.3 collective-permute-start.11
  100.4 0.8 fusion
  101.3 3.4 %collective-permute-done.11 = bf16[1,4,1,8,128]{4,3,2,1,0:T(8,128)(2,1)S(1)} collective-permute-done((bf16[1,4,1,8,128]{4,3,2,1,0:T(8,128)(2,1)S(1)}, bf16[1,4,1,8,128]{4,3,2,1,0:T(8,128)(2,1)S(1)}, u32[]{:S(2)}, u32[]{:S(2)}) %collective-permute-start.11) | collective-permute-done | bytes 8224 | tf_op jit(solution)/shard_map/ppermute | solution.py:16
  109.0 0.8 fusion.34
  109.8 74.2 %all-reduce.7.cloned.1.call-done = f32[3,3,3,128,128]{4,3,2,1,0:T(8,128)} async-done(((f32[3,3,3,128,128]{4,3,2,1,0:T(8,128)}), f32[3,3,3,128,128]{4,3,2,1,0:T(8,128)}) %all-reduce.7.cloned.1.call-update) | async-done | bytes 1769488 | tf_op jit(solution)/shard_map/psum | solution.py:120
  184.0 2.6 multiply_convert_fusion.1
  186.6 83.0 %all-reduce.9.cloned.1.call-done = f32[3,3,3,128,256]{4,3,2,1,0:T(8,128)} async-done(((f32[3,3,3,128,256]{4,3,2,1,0:T(8,128)}), f32[3,3,3,128,256]{4,3,2,1,0:T(8,128)}) %all-reduce.9.cloned.1.call-update) | async-done | bytes 3538960 | tf_op jit(solution)/shard_map/psum | solution.py:122
  269.6 3.7 %multiply_convert_fusion = bf16[3,3,3,128,256]{4,3,2,1,0:T(8,128)(2,1)} fusion(f32[3,3,3,128,256]{4,3,2,1,0:T(8,128)} %all-reduce.9.cloned.1.call-done), kind=kLoop, calls=%fused_computation | loop fusion | flops 1769472 | bytes 5308416 | tf_op jit(solution)/shard_map/convert_element_type | solution.py:123
  (207 shorter events, 24.9 us)
Async XLA Ops:
  7.2 70.8 %reduce-scatter.2.cloned.1.call-start = ((), (), s32[]{:S(2)}) async-start(), calls=%async_computation.1 | async-start | bytes 49152 | tf_op jit(solution)/shard_map/reduce_scatter | solution.py:113
  8.0 10.2 %collective-permute-start = (bf16[1,1,16,8,128]{4,3,2,1,0:T(8,128)(2,1)S(1)}, bf16[1,1,16,8,128]{4,3,2,1,0:T(8,128)(2,1)S(1)}, u32[]{:S(2)}, u32[]{:S(2)}) collective-permute-start(bf16[1,1,16,8,128]{4,3,2,1,0:T(8,128)(2,1)S(1)} %get-tuple-element.12), channel_id=1, source_target_pairs={{0,4},{4,8},{8,12},{1,5},{5,9},{9,13},{2,6},{6,10},{10,14},{3,7},{... | collective-permute-start | bytes 98312 | tf_op jit(solution)/shard_map/ppermute | solution.py:13
  12.9 5.3 %copy-start.3 = (bf16[1,2,16,8,128]{4,3,2,1,0:T(8,128)(2,1)S(1)}, bf16[1,2,16,8,128]{4,3,2,1,0:T(8,128)(2,1)}, u32[]{:S(2)}) copy-start(bf16[1,2,16,8,128]{4,3,2,1,0:T(8,128)(2,1)} %param.4) | copy-start | bytes 196612
  12.9 5.9 %collective-permute-start.1 = (bf16[1,1,16,8,128]{4,3,2,1,0:T(8,128)(2,1)S(1)}, bf16[1,1,16,8,128]{4,3,2,1,0:T(8,128)(2,1)S(1)}, u32[]{:S(2)}, u32[]{:S(2)}) collective-permute-start(bf16[1,1,16,8,128]{4,3,2,1,0:T(8,128)(2,1)S(1)} %get-tuple-element.11), channel_id=1, source_target_pairs={{4,0},{8,4},{12,8},{5,1},{9,5},{13,9},{6,2},{10,6},{14,10},{7,3},{... | collective-permute-start | bytes 98312 | tf_op jit(solution)/shard_map/ppermute | solution.py:16
  18.2 11.2 %copy-start.13 = (bf16[1,1,16,8,128]{4,3,2,1,0:T(8,128)(2,1)}, bf16[1,1,16,8,128]{4,3,2,1,0:T(8,128)(2,1)S(1)}, u32[]{:S(2)}) copy-start(bf16[1,1,16,8,128]{4,3,2,1,0:T(8,128)(2,1)S(1)} %collective-permute-done) | copy-start | bytes 98308
  18.9 13.1 %copy-start.11 = (bf16[1,1,16,8,128]{4,3,2,1,0:T(8,128)(2,1)}, bf16[1,1,16,8,128]{4,3,2,1,0:T(8,128)(2,1)S(1)}, u32[]{:S(2)}) copy-start(bf16[1,1,16,8,128]{4,3,2,1,0:T(8,128)(2,1)S(1)} %collective-permute-done.1) | copy-start | bytes 98308
  18.9 8.1 %collective-permute-start.2 = (bf16[1,4,1,8,128]{4,3,2,1,0:T(8,128)(2,1)S(1)}, bf16[1,4,1,8,128]{4,3,2,1,0:T(8,128)(2,1)S(1)}, u32[]{:S(2)}, u32[]{:S(2)}) collective-permute-start(bf16[1,4,1,8,128]{4,3,2,1,0:T(8,128)(2,1)S(1)} %get-tuple-element.7), channel_id=1, source_target_pairs={{0,2},{1,3},{4,6},{5,7},{8,10},{9,11},{12,14},{13,15},{16,18},{17,... | collective-permute-start | bytes 24584 | tf_op jit(solution)/shard_map/ppermute | solution.py:13
  22.3 3.0 %copy-start.2 = (bf16[3,3,3,128,128]{4,3,2,1,0:T(8,128)(2,1)S(1)}, bf16[3,3,3,128,128]{4,3,2,1,0:T(8,128)(2,1)}, u32[]{:S(2)}) copy-start(bf16[3,3,3,128,128]{4,3,2,1,0:T(8,128)(2,1)} %param.5) | copy-start | bytes 2654212
  22.3 5.7 %collective-permute-start.3 = (bf16[1,4,1,8,128]{4,3,2,1,0:T(8,128)(2,1)S(1)}, bf16[1,4,1,8,128]{4,3,2,1,0:T(8,128)(2,1)S(1)}, u32[]{:S(2)}, u32[]{:S(2)}) collective-permute-start(bf16[1,4,1,8,128]{4,3,2,1,0:T(8,128)(2,1)S(1)} %get-tuple-element.8), channel_id=1, source_target_pairs={{2,0},{3,1},{6,4},{7,5},{10,8},{11,9},{14,12},{15,13},{18,16},{19,... | collective-permute-start | bytes 24584 | tf_op jit(solution)/shard_map/ppermute | solution.py:16
  27.0 4.6 %copy-start.9 = (bf16[1,4,1,8,128]{4,3,2,1,0:T(8,128)(2,1)}, bf16[1,4,1,8,128]{4,3,2,1,0:T(8,128)(2,1)S(1)}, u32[]{:S(2)}) copy-start(bf16[1,4,1,8,128]{4,3,2,1,0:T(8,128)(2,1)S(1)} %collective-permute-done.2) | copy-start | bytes 24580
  28.0 4.3 %copy-start.7 = (bf16[1,4,1,8,128]{4,3,2,1,0:T(8,128)(2,1)}, bf16[1,4,1,8,128]{4,3,2,1,0:T(8,128)(2,1)S(1)}, u32[]{:S(2)}) copy-start(bf16[1,4,1,8,128]{4,3,2,1,0:T(8,128)(2,1)S(1)} %collective-permute-done.3) | copy-start | bytes 24580
  32.5 14.1 %copy-start = (bf16[3,3,3,128,256]{4,3,2,1,0:T(8,128)(2,1)S(1)}, bf16[3,3,3,128,256]{4,3,2,1,0:T(8,128)(2,1)}, u32[]{:S(2)}) copy-start(bf16[3,3,3,128,256]{4,3,2,1,0:T(8,128)(2,1)} %param.6) | copy-start | bytes 5308420
  37.0 6.5 %collective-permute-start.4 = (bf16[1,1,16,4,128]{4,2,3,1,0:T(8,128)(2,1)S(1)}, bf16[1,1,16,4,128]{4,2,3,1,0:T(8,128)(2,1)S(1)}, u32[]{:S(2)}, u32[]{:S(2)}) collective-permute-start(bf16[1,1,16,4,128]{4,2,3,1,0:T(8,128)(2,1)S(1)} %bitcast.1506), channel_id=1, source_target_pairs={{0,4},{4,8},{8,12},{1,5},{5,9},{9,13},{2,6},{6,10},{10,14},{3,7},{... | collective-permute-start | bytes 49160 | tf_op jit(solution)/shard_map/ppermute | solution.py:13
  41.0 5.6 %collective-permute-start.5 = (bf16[1,1,16,4,128]{4,2,3,1,0:T(8,128)(2,1)S(1)}, bf16[1,1,16,4,128]{4,2,3,1,0:T(8,128)(2,1)S(1)}, u32[]{:S(2)}, u32[]{:S(2)}) collective-permute-start(bf16[1,1,16,4,128]{4,2,3,1,0:T(8,128)(2,1)S(1)} %bitcast.1507), channel_id=1, source_target_pairs={{4,0},{8,4},{12,8},{5,1},{9,5},{13,9},{6,2},{10,6},{14,10},{7,3},{... | collective-permute-start | bytes 49160 | tf_op jit(solution)/shard_map/ppermute | solution.py:16
  48.0 2.3 copy-start.15
  50.5 9.6 %collective-permute-start.6 = (bf16[1,1,16,4,256]{4,2,3,1,0:T(8,128)(2,1)S(1)}, bf16[1,1,16,4,256]{4,2,3,1,0:T(8,128)(2,1)S(1)}, u32[]{:S(2)}, u32[]{:S(2)}) collective-permute-start(bf16[1,1,16,4,256]{4,2,3,1,0:T(8,128)(2,1)S(1)} %fusion.92), channel_id=1, source_target_pairs={{0,4},{4,8},{8,12},{1,5},{5,9},{9,13},{2,6},{6,10},{10,14},{3,7},{... | collective-permute-start | bytes 98312 | tf_op jit(solution)/shard_map/ppermute | solution.py:13
  54.0 7.9 %collective-permute-start.7 = (bf16[1,1,16,4,256]{4,2,3,1,0:T(8,128)(2,1)S(1)}, bf16[1,1,16,4,256]{4,2,3,1,0:T(8,128)(2,1)S(1)}, u32[]{:S(2)}, u32[]{:S(2)}) collective-permute-start(bf16[1,1,16,4,256]{4,2,3,1,0:T(8,128)(2,1)S(1)} %fusion.92), channel_id=1, source_target_pairs={{4,0},{8,4},{12,8},{5,1},{9,5},{13,9},{6,2},{10,6},{14,10},{7,3},{... | collective-permute-start | bytes 98312 | tf_op jit(solution)/shard_map/ppermute | solution.py:16
  60.1 1.8 copy-start.1
  66.4 117.6 %all-reduce.7.cloned.1.call-start = ((), (), s32[]{:S(2)}) async-start(), calls=%async_computation.2 | async-start | bytes 3538944 | tf_op jit(solution)/shard_map/psum | solution.py:120
  78.8 6.6 %copy-start.5 = (bf16[2,16,8,128]{3,2,1,0:T(8,128)(2,1)}, bf16[2,16,8,128]{3,2,1,0:T(8,128)(2,1)S(1)}, u32[]{:S(2)}) copy-start(bf16[2,16,8,128]{3,2,1,0:T(8,128)(2,1)S(1)} %fusion.84) | copy-start | bytes 196612
  78.8 1.6 copy-start.14
  80.2 0.9 copy-start.8
  80.9 0.9 copy-start.10
  83.6 0.9 copy-start.12
  85.6 1.2 copy-start.4
  86.8 182.8 %all-reduce.9.cloned.1.call-start = ((), (), s32[]{:S(2)}) async-start(), calls=%async_computation.3 | async-start | bytes 7077888 | tf_op jit(solution)/shard_map/psum | solution.py:122
  87.0 5.6 %collective-permute-start.8 = (bf16[1,1,16,8,128]{4,3,2,1,0:T(8,128)(2,1)S(1)}, bf16[1,1,16,8,128]{4,3,2,1,0:T(8,128)(2,1)S(1)}, u32[]{:S(2)}, u32[]{:S(2)}) collective-permute-start(bf16[1,1,16,8,128]{4,3,2,1,0:T(8,128)(2,1)S(1)} %get-tuple-element.9), channel_id=1, source_target_pairs={{0,4},{4,8},{8,12},{1,5},{5,9},{9,13},{2,6},{6,10},{10,14},{3,7},{... | collective-permute-start | bytes 98312 | tf_op jit(solution)/shard_map/ppermute | solution.py:13
  90.4 6.0 %collective-permute-start.9 = (bf16[1,1,16,8,128]{4,3,2,1,0:T(8,128)(2,1)S(1)}, bf16[1,1,16,8,128]{4,3,2,1,0:T(8,128)(2,1)S(1)}, u32[]{:S(2)}, u32[]{:S(2)}) collective-permute-start(bf16[1,1,16,8,128]{4,3,2,1,0:T(8,128)(2,1)S(1)} %get-tuple-element.10), channel_id=1, source_target_pairs={{4,0},{8,4},{12,8},{5,1},{9,5},{13,9},{6,2},{10,6},{14,10},{7,3},{... | collective-permute-start | bytes 98312 | tf_op jit(solution)/shard_map/ppermute | solution.py:16
  96.4 4.9 %collective-permute-start.10 = (bf16[1,4,1,8,128]{4,3,2,1,0:T(8,128)(2,1)S(1)}, bf16[1,4,1,8,128]{4,3,2,1,0:T(8,128)(2,1)S(1)}, u32[]{:S(2)}, u32[]{:S(2)}) collective-permute-start(bf16[1,4,1,8,128]{4,3,2,1,0:T(8,128)(2,1)S(1)} %get-tuple-element.5), channel_id=1, source_target_pairs={{0,2},{1,3},{4,6},{5,7},{8,10},{9,11},{12,14},{13,15},{16,18},{17,... | collective-permute-start | bytes 24584 | tf_op jit(solution)/shard_map/ppermute | solution.py:13
  99.1 5.5 %collective-permute-start.11 = (bf16[1,4,1,8,128]{4,3,2,1,0:T(8,128)(2,1)S(1)}, bf16[1,4,1,8,128]{4,3,2,1,0:T(8,128)(2,1)S(1)}, u32[]{:S(2)}, u32[]{:S(2)}) collective-permute-start(bf16[1,4,1,8,128]{4,3,2,1,0:T(8,128)(2,1)S(1)} %get-tuple-element.6), channel_id=1, source_target_pairs={{2,0},{3,1},{6,4},{7,5},{10,8},{11,9},{14,12},{15,13},{18,16},{19,... | collective-permute-start | bytes 24584 | tf_op jit(solution)/shard_map/ppermute | solution.py:16
  105.5 1.4 copy-start.6
Sparse Core Ops, SparseCore 0:
  66.6 11.3 reduce-scatter.1
  87.0 96.9 all-reduce.6
  186.5 83.0 all-reduce.8
where the time goes:
time: 281 us; the launch traced here: 280 us
  waiting for transfers between devices  180 us (64%)
  matrix products  31.2 us (11%)
  starting transfers between devices  30 us (11%)
  between operations  14.4 us (5%)
  local copies, waits for them, and re-layouts  12.3 us (4%)
  other arithmetic  7.75 us (3%)
  blocking collectives  4.48 us (2%)
    psum x1, waiting for transfers between devices, per_device(): late_total = lax.psum(late_part, ('space', 'rep'))  83 us
    psum x1, waiting for transfers between devices, per_device(): early_total = lax.psum(early_part, ('space', 'chan', 'rep'))  74.2 us
    ppermute x6, starting transfers between devices, padded_2(): lax.ppermute(lax.slice_in_dim(block, block.shape[dim] - width, None, axis...  21.8 us
    dot_general x108, matrix products, conv_padded(): jnp.einsum('sxyzc,co->sxyzo', window, weight[first, second, third], prefe...  17.4 us
    dot_general x54, matrix products, kernel_grad(): jnp.einsum('sxyzc,sxyzo->co', window, delta, preferred_element_type=jnp.f...  13.9 us
    ppermute x6, waiting for transfers between devices, padded_2(): lax.ppermute(lax.slice_in_dim(block, 0, width, axis=dim), axis, backward)  11.9 us
    reduce_scatter x1, waiting for transfers between devices, per_device(): lax.psum_scatter(back_partial, 'chan', scatter_dimension=2, tiled=True)  10.6 us
    unnamed x36, local copies, waits for them, and re-layouts  8.58 us
  transfers between devices with their start and end apart: 15, of which 8 were waited for; matrix products, arithmetic and copies ran while one was open for 8% of the time, Pallas kernels for 0%

commit v1 on v0

--- a/solution.py
+++ b/solution.py
@@ -119,7 +119,7 @@
     )
     early_total = lax.psum(early_part, ("space", "chan", "rep"))
     grad_early = (early_total * scale).astype(jnp.bfloat16)
-    late_total = lax.psum(late_part, ("space", "rep"))
+    late_total = lax.psum(lax.psum(late_part, "rep"), "space")
     grad_late = (late_total * scale).astype(jnp.bfloat16)
     return (grad_early, grad_late, grad_volume)
 

time: 281 us -> 345 us (1.23)
  waiting for transfers between devices: 180 us -> 244 us
    psum x1 -> x2, waiting for transfers between devices: 83 us -> 132 us  [per_device(): late_total = lax.psum(lax.psum(late_part, 'rep'), 'space')]
    psum x1, waiting for transfers between devices: 74.2 us -> 94.1 us  [per_device(): early_total = lax.psum(early_part, ('space', 'chan', 'rep'))]
    ppermute x6, waiting for transfers between devices: 11.9 us -> 7.4 us  [padded_2(): lax.ppermute(lax.slice_in_dim(block, 0, width, axis=dim), axis, backward)]
    unnamed x36 -> x20, local copies, waits for them, and re-layouts: 8.58 us -> 8.54 us
  transfers between devices with their start and end apart: 15 -> 16, of which waited for: 8 -> 7; matrix products, arithmetic and copies ran while one was open for 8% -> 8% of each run, Pallas kernels for 0% -> 0%
where the time goes in v1:
time: 345 us; the launch traced here: 344 us
  waiting for transfers between devices  244 us (71%)
  starting transfers between devices  29.8 us (9%)
  matrix products  29.3 us (8%)
  between operations  16.2 us (5%)
  local copies, waits for them, and re-layouts  12.2 us (4%)
  other arithmetic  7.75 us (2%)
  blocking collectives  4.48 us (1%)
    psum x2, waiting for transfers between devices, per_device(): late_total = lax.psum(lax.psum(late_part, 'rep'), 'space')  132 us
    psum x1, waiting for transfers between devices, per_device(): early_total = lax.psum(early_part, ('space', 'chan', 'rep'))  94.1 us
    ppermute x6, starting transfers between devices, padded_2(): lax.ppermute(lax.slice_in_dim(block, block.shape[dim] - width, None, axis...  21.6 us
    dot_general x108, matrix products, conv_padded(): jnp.einsum('sxyzc,co->sxyzo', window, weight[first, second, third], prefe...  17.4 us
    dot_general x54, matrix products, kernel_grad(): jnp.einsum('sxyzc,sxyzo->co', window, delta, preferred_element_type=jnp.f...  11.9 us
    reduce_scatter x1, waiting for transfers between devices, per_device(): lax.psum_scatter(back_partial, 'chan', scatter_dimension=2, tiled=True)  10.5 us
    unnamed x20, local copies, waits for them, and re-layouts  8.54 us
    ppermute x6, starting transfers between devices, padded_2(): lax.ppermute(lax.slice_in_dim(block, 0, width, axis=dim), axis, backward)  8.02 us
  transfers between devices with their start and end apart: 16, of which 7 were waited for; matrix products, arithmetic and copies ran while one was open for 8% of the time, Pallas kernels for 0%

profile of v1, /device:TPU:0, one launch (start us, length us, event | category | flops | bytes accessed | tf_op | source)
XLA Modules:
  0.0 344.0 jit_solution(1736699580166071902)
XLA Ops:
  8.0 0.8 fusion.308
  8.8 4.9 %collective-permute-start = (bf16[1,1,16,8,128]{4,3,2,1,0:T(8,128)(2,1)S(1)}, bf16[1,1,16,8,128]{4,3,2,1,0:T(8,128)(2,1)S(1)}, u32[]{:S(2)}, u32[]{:S(2)}) collective-permute-start(bf16[1,1,16,8,128]{4,3,2,1,0:T(8,128)(2,1)S(1)} %get-tuple-element.12), channel_id=1, source_target_pairs={{0,4},{4,8},{8,12},{1,5},{5,9},{9,13},{2,6},{6,10},{10,14},{3,7},{... | collective-permute-start | bytes 98312 | tf_op jit(solution)/shard_map/ppermute | solution.py:13
  13.8 1.4 collective-permute-start.1
  15.2 3.8 %copy.129 = bf16[3,3,3,128,256]{3,4,2,1,0:T(8,128)(2,1)} copy(bf16[3,3,3,128,256]{4,3,2,1,0:T(8,128)(2,1)} %param.6) | data formatting | bytes 3538944 | tf_op args[2]
  19.1 0.6 collective-permute-done.1
  19.7 3.4 collective-permute-start.2
  23.1 1.4 collective-permute-start.3
  24.6 1.6 reverse_bitcast_fusion
  26.2 1.7 copy.133
  27.8 1.0 collective-permute-done.3
  33.4 4.5 %all-gather = bf16[16,4,128]{2,0,1:T(8,128)(2,1)S(1)} all-gather(bf16[8,4,128]{2,0,1:T(8,128)(2,1)S(1)} %fusion.279), channel_id=2, replica_groups=mesh['groups'=2,'space'=4,'chan'=2,'rep'=2] {'chan'}, dimensions={0}, use_global_device_ids=true | all-gather | bytes 24576 | tf_op jit(solution)/shard_map/all_gather | solution.py:111
  37.9 3.9 %collective-permute-start.4 = (bf16[1,1,16,4,128]{4,2,3,1,0:T(8,128)(2,1)S(1)}, bf16[1,1,16,4,128]{4,2,3,1,0:T(8,128)(2,1)S(1)}, u32[]{:S(2)}, u32[]{:S(2)}) collective-permute-start(bf16[1,1,16,4,128]{4,2,3,1,0:T(8,128)(2,1)S(1)} %bitcast.1506), channel_id=1, source_target_pairs={{0,4},{4,8},{8,12},{1,5},{5,9},{9,13},{2,6},{6,10},{10,14},{3,7},{... | collective-permute-start | bytes 49160 | tf_op jit(solution)/shard_map/ppermute | solution.py:13
  41.8 1.3 collective-permute-start.5
  43.1 1.3 reverse_bitcast_fusion.1
  44.4 3.1 collective-permute-done.5
  51.3 3.5 %collective-permute-start.6 = (bf16[1,1,16,4,256]{4,2,3,1,0:T(8,128)(2,1)S(1)}, bf16[1,1,16,4,256]{4,2,3,1,0:T(8,128)(2,1)S(1)}, u32[]{:S(2)}, u32[]{:S(2)}) collective-permute-start(bf16[1,1,16,4,256]{4,2,3,1,0:T(8,128)(2,1)S(1)} %fusion.92), channel_id=1, source_target_pairs={{0,4},{4,8},{8,12},{1,5},{5,9},{9,13},{2,6},{6,10},{10,14},{3,7},{... | collective-permute-start | bytes 98312 | tf_op jit(solution)/shard_map/ppermute | solution.py:13
  54.8 1.3 collective-permute-start.7
  61.4 1.8 copy-done.1
  66.9 0.8 fusion.64
  67.7 0.9 fusion
  68.7 10.5 %reduce-scatter.2.cloned.1.call-done = f32[1,1,8,4,128]{4,2,3,1,0:T(8,128)} async-done(((f32[1,1,16,4,128]{4,2,3,1,0:T(8,128)}), f32[1,1,8,4,128]{4,2,3,1,0:T(8,128)}) %reduce-scatter.2.cloned.1.call-update) | async-done | bytes 16400 | tf_op jit(solution)/shard_map/reduce_scatter | solution.py:113
  79.1 0.7 multiply_bitcast_fusion.1
  80.1 3.4 collective-permute-start.8
  83.6 1.3 collective-permute-start.9
  84.9 0.2 fusion.61
  85.1 0.2 fusion.60
  85.3 0.2 fusion.59
  85.5 0.2 fusion.58
  85.8 0.2 fusion.57
  86.0 0.2 fusion.56
  86.4 0.2 fusion.54
  86.7 0.2 fusion.53
  87.1 0.2 fusion.51
  87.3 0.2 fusion.50
  87.5 0.2 fusion.49
  87.8 0.2 fusion.48
  88.4 0.2 fusion.45
  89.1 0.2 fusion.42
  89.8 0.2 fusion.39
  90.7 2.5 collective-permute-start.10
  93.2 1.3 collective-permute-start.11
  94.7 1.2 copy-done.4
  96.0 2.7 collective-permute-done.11
  103.1 0.8 fusion.34
  103.9 94.1 %all-reduce.8.cloned.1.call-done = f32[3,3,3,128,128]{4,3,2,1,0:T(8,128)} async-done(((f32[3,3,3,128,128]{4,3,2,1,0:T(8,128)}), f32[3,3,3,128,128]{4,3,2,1,0:T(8,128)}) %all-reduce.8.cloned.1.call-update) | async-done | bytes 1769488 | tf_op jit(solution)/shard_map/psum | solution.py:120
  198.0 2.6 multiply_convert_fusion.1
  200.6 132.1 %all-reduce.12.cloned.1.call-done = f32[3,3,3,128,256]{4,3,2,1,0:T(8,128)} async-done(((f32[3,3,3,128,256]{4,3,2,1,0:T(8,128)}), f32[3,3,3,128,256]{4,3,2,1,0:T(8,128)}) %all-reduce.12.cloned.1.call-update) | async-done | bytes 3538960 | tf_op jit(solution)/shard_map/psum | solution.py:122
  332.7 3.7 %multiply_convert_fusion = bf16[3,3,3,128,256]{4,3,2,1,0:T(8,128)(2,1)} fusion(f32[3,3,3,128,256]{4,3,2,1,0:T(8,128)} %all-reduce.12.cloned.1.call-done), kind=kLoop, calls=%fused_computation | loop fusion | flops 1769472 | bytes 5308416 | tf_op jit(solution)/shard_map/convert_element_type | solution.py:123
  (194 shorter events, 24.8 us)
Async XLA Ops:
  8.0 71.1 %reduce-scatter.2.cloned.1.call-start = ((), (), s32[]{:S(2)}) async-start(), calls=%async_computation.1 | async-start | bytes 49152 | tf_op jit(solution)/shard_map/reduce_scatter | solution.py:113
  8.8 10.2 %collective-permute-start = (bf16[1,1,16,8,128]{4,3,2,1,0:T(8,128)(2,1)S(1)}, bf16[1,1,16,8,128]{4,3,2,1,0:T(8,128)(2,1)S(1)}, u32[]{:S(2)}, u32[]{:S(2)}) collective-permute-start(bf16[1,1,16,8,128]{4,3,2,1,0:T(8,128)(2,1)S(1)} %get-tuple-element.12), channel_id=1, source_target_pairs={{0,4},{4,8},{8,12},{1,5},{5,9},{9,13},{2,6},{6,10},{10,14},{3,7},{... | collective-permute-start | bytes 98312 | tf_op jit(solution)/shard_map/ppermute | solution.py:13
  13.8 5.3 %copy-start.3 = (bf16[1,2,16,8,128]{4,3,2,1,0:T(8,128)(2,1)S(1)}, bf16[1,2,16,8,128]{4,3,2,1,0:T(8,128)(2,1)}, u32[]{:S(2)}) copy-start(bf16[1,2,16,8,128]{4,3,2,1,0:T(8,128)(2,1)} %param.4) | copy-start | bytes 196612
  13.8 5.9 %collective-permute-start.1 = (bf16[1,1,16,8,128]{4,3,2,1,0:T(8,128)(2,1)S(1)}, bf16[1,1,16,8,128]{4,3,2,1,0:T(8,128)(2,1)S(1)}, u32[]{:S(2)}, u32[]{:S(2)}) collective-permute-start(bf16[1,1,16,8,128]{4,3,2,1,0:T(8,128)(2,1)S(1)} %get-tuple-element.11), channel_id=1, source_target_pairs={{4,0},{8,4},{12,8},{5,1},{9,5},{13,9},{6,2},{10,6},{14,10},{7,3},{... | collective-permute-start | bytes 98312 | tf_op jit(solution)/shard_map/ppermute | solution.py:16
  19.0 11.2 %copy-start.5 = (bf16[1,1,16,8,128]{4,3,2,1,0:T(8,128)(2,1)}, bf16[1,1,16,8,128]{4,3,2,1,0:T(8,128)(2,1)S(1)}, u32[]{:S(2)}) copy-start(bf16[1,1,16,8,128]{4,3,2,1,0:T(8,128)(2,1)S(1)} %collective-permute-done) | copy-start | bytes 98308
  19.7 8.1 %collective-permute-start.2 = (bf16[1,4,1,8,128]{4,3,2,1,0:T(8,128)(2,1)S(1)}, bf16[1,4,1,8,128]{4,3,2,1,0:T(8,128)(2,1)S(1)}, u32[]{:S(2)}, u32[]{:S(2)}) collective-permute-start(bf16[1,4,1,8,128]{4,3,2,1,0:T(8,128)(2,1)S(1)} %get-tuple-element.7), channel_id=1, source_target_pairs={{0,2},{1,3},{4,6},{5,7},{8,10},{9,11},{12,14},{13,15},{16,18},{17,... | collective-permute-start | bytes 24584 | tf_op jit(solution)/shard_map/ppermute | solution.py:13
  23.1 3.0 copy-start.2
  23.1 5.7 %collective-permute-start.3 = (bf16[1,4,1,8,128]{4,3,2,1,0:T(8,128)(2,1)S(1)}, bf16[1,4,1,8,128]{4,3,2,1,0:T(8,128)(2,1)S(1)}, u32[]{:S(2)}, u32[]{:S(2)}) collective-permute-start(bf16[1,4,1,8,128]{4,3,2,1,0:T(8,128)(2,1)S(1)} %get-tuple-element.8), channel_id=1, source_target_pairs={{2,0},{3,1},{6,4},{7,5},{10,8},{11,9},{14,12},{15,13},{18,16},{19,... | collective-permute-start | bytes 24584 | tf_op jit(solution)/shard_map/ppermute | solution.py:16
  33.3 14.1 %copy-start = (bf16[3,3,3,128,256]{4,3,2,1,0:T(8,128)(2,1)S(1)}, bf16[3,3,3,128,256]{4,3,2,1,0:T(8,128)(2,1)}, u32[]{:S(2)}) copy-start(bf16[3,3,3,128,256]{4,3,2,1,0:T(8,128)(2,1)} %param.6) | copy-start | bytes 5308420
  37.9 6.5 %collective-permute-start.4 = (bf16[1,1,16,4,128]{4,2,3,1,0:T(8,128)(2,1)S(1)}, bf16[1,1,16,4,128]{4,2,3,1,0:T(8,128)(2,1)S(1)}, u32[]{:S(2)}, u32[]{:S(2)}) collective-permute-start(bf16[1,1,16,4,128]{4,2,3,1,0:T(8,128)(2,1)S(1)} %bitcast.1506), channel_id=1, source_target_pairs={{0,4},{4,8},{8,12},{1,5},{5,9},{9,13},{2,6},{6,10},{10,14},{3,7},{... | collective-permute-start | bytes 49160 | tf_op jit(solution)/shard_map/ppermute | solution.py:13
  41.8 5.6 %collective-permute-start.5 = (bf16[1,1,16,4,128]{4,2,3,1,0:T(8,128)(2,1)S(1)}, bf16[1,1,16,4,128]{4,2,3,1,0:T(8,128)(2,1)S(1)}, u32[]{:S(2)}, u32[]{:S(2)}) collective-permute-start(bf16[1,1,16,4,128]{4,2,3,1,0:T(8,128)(2,1)S(1)} %bitcast.1507), channel_id=1, source_target_pairs={{4,0},{8,4},{12,8},{5,1},{9,5},{13,9},{6,2},{10,6},{14,10},{7,3},{... | collective-permute-start | bytes 49160 | tf_op jit(solution)/shard_map/ppermute | solution.py:16
  48.9 2.3 copy-start.7
  51.3 10.0 %collective-permute-start.6 = (bf16[1,1,16,4,256]{4,2,3,1,0:T(8,128)(2,1)S(1)}, bf16[1,1,16,4,256]{4,2,3,1,0:T(8,128)(2,1)S(1)}, u32[]{:S(2)}, u32[]{:S(2)}) collective-permute-start(bf16[1,1,16,4,256]{4,2,3,1,0:T(8,128)(2,1)S(1)} %fusion.92), channel_id=1, source_target_pairs={{0,4},{4,8},{8,12},{1,5},{5,9},{9,13},{2,6},{6,10},{10,14},{3,7},{... | collective-permute-start | bytes 98312 | tf_op jit(solution)/shard_map/ppermute | solution.py:13
  54.8 8.3 %collective-permute-start.7 = (bf16[1,1,16,4,256]{4,2,3,1,0:T(8,128)(2,1)S(1)}, bf16[1,1,16,4,256]{4,2,3,1,0:T(8,128)(2,1)S(1)}, u32[]{:S(2)}, u32[]{:S(2)}) collective-permute-start(bf16[1,1,16,4,256]{4,2,3,1,0:T(8,128)(2,1)S(1)} %fusion.92), channel_id=1, source_target_pairs={{4,0},{8,4},{12,8},{5,1},{9,5},{13,9},{6,2},{10,6},{14,10},{7,3},{... | collective-permute-start | bytes 98312 | tf_op jit(solution)/shard_map/ppermute | solution.py:16
  61.3 1.8 copy-start.1
  67.7 33.2 %all-reduce.10.cloned.1.call-start = ((), (), s32[]{:S(2)}) async-start(), calls=%async_computation.3 | async-start | bytes 7077888 | tf_op jit(solution)/shard_map/psum | solution.py:122
  68.6 129.4 %all-reduce.8.cloned.1.call-start = ((), (), s32[]{:S(2)}) async-start(), calls=%async_computation.2 | async-start | bytes 3538944 | tf_op jit(solution)/shard_map/psum | solution.py:120
  80.1 10.5 %collective-permute-start.8 = (bf16[1,1,16,8,128]{4,3,2,1,0:T(8,128)(2,1)S(1)}, bf16[1,1,16,8,128]{4,3,2,1,0:T(8,128)(2,1)S(1)}, u32[]{:S(2)}, u32[]{:S(2)}) collective-permute-start(bf16[1,1,16,8,128]{4,3,2,1,0:T(8,128)(2,1)S(1)} %get-tuple-element.9), channel_id=1, source_target_pairs={{0,4},{4,8},{8,12},{1,5},{5,9},{9,13},{2,6},{6,10},{10,14},{3,7},{... | collective-permute-start | bytes 98312 | tf_op jit(solution)/shard_map/ppermute | solution.py:13
  83.6 2.2 copy-start.6
  83.6 7.1 %collective-permute-start.9 = (bf16[1,1,16,8,128]{4,3,2,1,0:T(8,128)(2,1)S(1)}, bf16[1,1,16,8,128]{4,3,2,1,0:T(8,128)(2,1)S(1)}, u32[]{:S(2)}, u32[]{:S(2)}) collective-permute-start(bf16[1,1,16,8,128]{4,3,2,1,0:T(8,128)(2,1)S(1)} %get-tuple-element.10), channel_id=1, source_target_pairs={{4,0},{8,4},{12,8},{5,1},{9,5},{13,9},{6,2},{10,6},{14,10},{7,3},{... | collective-permute-start | bytes 98312 | tf_op jit(solution)/shard_map/ppermute | solution.py:16
  90.7 5.3 %collective-permute-start.10 = (bf16[1,4,1,8,128]{4,3,2,1,0:T(8,128)(2,1)S(1)}, bf16[1,4,1,8,128]{4,3,2,1,0:T(8,128)(2,1)S(1)}, u32[]{:S(2)}, u32[]{:S(2)}) collective-permute-start(bf16[1,4,1,8,128]{4,3,2,1,0:T(8,128)(2,1)S(1)} %get-tuple-element.5), channel_id=1, source_target_pairs={{0,2},{1,3},{4,6},{5,7},{8,10},{9,11},{12,14},{13,15},{16,18},{17,... | collective-permute-start | bytes 24584 | tf_op jit(solution)/shard_map/ppermute | solution.py:13
  93.2 5.5 %collective-permute-start.11 = (bf16[1,4,1,8,128]{4,3,2,1,0:T(8,128)(2,1)S(1)}, bf16[1,4,1,8,128]{4,3,2,1,0:T(8,128)(2,1)S(1)}, u32[]{:S(2)}, u32[]{:S(2)}) collective-permute-start(bf16[1,4,1,8,128]{4,3,2,1,0:T(8,128)(2,1)S(1)} %get-tuple-element.6), channel_id=1, source_target_pairs={{2,0},{3,1},{6,4},{7,5},{10,8},{11,9},{14,12},{15,13},{18,16},{19,... | collective-permute-start | bytes 24584 | tf_op jit(solution)/shard_map/ppermute | solution.py:16
  94.7 1.2 copy-start.4
  95.9 236.8 %all-reduce.12.cloned.1.call-start = ((), (), s32[]{:S(2)}) async-start(), calls=%async_computation.4 | async-start | bytes 7077888 | tf_op jit(solution)/shard_map/psum | solution.py:122
Sparse Core Ops, SparseCore 0:
  67.8 11.2 reduce-scatter.1
Sparse Core Ops, SparseCore 1:
  70.5 25.3 all-reduce.9
  100.2 97.7 all-reduce.7
  200.2 132.5 all-reduce.11
